TPU v7x, 32 devices: a whole 2x2x4 slice. The times are simulated.
32 devices in a mesh: replica: 16 (over z, x, core), shard: 2 (over y).
Axes of the slice: x: 2, y: 2, z: 4, core: 2. Of those that a mesh axis runs over, the one named last changes fastest.
Arguments:
- tokens: bfloat16 [8192, 768], P(('replica', 'shard')), may hold values from -32 to 32
- lengths: int32 [32], P(('replica', 'shard')), may hold values from 1 to 256, 5120 in all
- cotangent: bfloat16 [8192, 768], P(('replica', 'shard')), may hold values from -6 to 6
- w_qkv: bfloat16 [768, 2304], P('shard'), may hold values from -0.14433757 to 0.14433757
- bias_q: bfloat16 [768], P('shard'), may hold values from -3 to 3
- bias_v: bfloat16 [768], P('shard'), may hold values from -3 to 3
- w_out: bfloat16 [768, 768], P('shard'), may hold values from -1.75 to 1.75
- bias_out: bfloat16 [768], P('shard'), may hold values from -3 to 3
- gain_attn: bfloat16 [768], P('shard'), may hold values from 0.5 to 1.5
- shift_attn: bfloat16 [768], P('shard'), may hold values from -3 to 3
- w_in: bfloat16 [768, 3072], P('shard'), may hold values from -0.21875 to 0.21875
- bias_in: bfloat16 [3072], P('shard'), may hold values from -3 to 3
- w_back: bfloat16 [3072, 768], P('shard'), may hold values from -0.109375 to 0.109375
- bias_back: bfloat16 [768], P('shard'), may hold values from -3 to 3
- gain_ffn: bfloat16 [768], P('shard'), may hold values from 0.5 to 1.5
- shift_ffn: bfloat16 [768], P('shard'), may hold values from -3 to 3
Outputs:
- block_out: bfloat16 [8192, 768], P(('replica', 'shard'))
- grad_tokens: float32 [8192, 768], P(('replica', 'shard'))
- grad_w_qkv: float32 [768, 2304], P('shard')
- grad_bias_q: float32 [768], P('shard')
- grad_bias_v: float32 [768], P('shard')
- grad_w_out: float32 [768, 768], P('shard')
- grad_bias_out: float32 [768], P('shard')
- grad_gain_attn: float32 [768], P('shard')
- grad_shift_attn: float32 [768], P('shard')
- grad_w_in: float32 [768, 3072], P('shard')
- grad_bias_in: float32 [3072], P('shard')
- grad_w_back: float32 [3072, 768], P('shard')
- grad_bias_back: float32 [768], P('shard')
- grad_gain_ffn: float32 [768], P('shard')
- grad_shift_ffn: float32 [768], P('shard')
Inputs may be any that keep to these rules, and one draw needn't show every extreme that they name: `lengths`: each sequence has at least one live token; the longest has exactly 256.
All inputs are finite; a program needn't handle non-finite values. No bound on the sum of `lengths` on one device may be relied on, other than what follows from the above.
Results may differ from a plain program's by a relative error of at most 0.012.
The roundings to bfloat16 on the way count: a program that leaves them out, or rounds other values in their place, can miss the bound.
Values may be sent and summed in bfloat16 or wider, within the bound.
A program may use at most 192 MiB of HBM per device.

v0:
```python
import jax
import jax.numpy as jnp
from jax import lax
from jax.sharding import PartitionSpec as P

HEADS = 12
HEAD_DIM = 64


def product(form, left, right):
    return jnp.einsum(form, left, right, preferred_element_type=jnp.float32)


def normalize(hidden):
    average = jnp.mean(hidden, axis=-1, keepdims=True)
    centred = hidden - average
    inv_std = lax.rsqrt(jnp.mean(centred * centred, axis=-1, keepdims=True) + 1e-12)
    return (centred * inv_std, inv_std)


def norm_back(grad_in, normed, inv_std, gain):
    grad_norm = grad_in * gain
    return inv_std * (
        grad_norm
        - jnp.mean(grad_norm, axis=-1, keepdims=True)
        - normed * jnp.mean(grad_norm * normed, axis=-1, keepdims=True)
    )


def gelu_slope(pre):
    return (
        0.5 * (1.0 + lax.erf(pre * 0.7071067811865476))
        + pre * jnp.exp(-0.5 * pre * pre) * 0.3989422804014327
    )


def on_device(
    tokens,
    lengths,
    cotangent,
    w_qkv,
    bias_q,
    bias_v,
    w_out,
    bias_out,
    gain_attn,
    shift_attn,
    w_in,
    bias_in,
    w_back,
    bias_back,
    gain_ffn,
    shift_ffn,
):
    bf16 = jnp.bfloat16
    f32 = jnp.float32
    full = (
        lax.all_gather(w_qkv, "shard", axis=0, tiled=True),
        lax.all_gather(bias_q, "shard", axis=0, tiled=True),
        lax.all_gather(bias_v, "shard", axis=0, tiled=True),
        lax.all_gather(w_out, "shard", axis=0, tiled=True),
        lax.all_gather(bias_out, "shard", axis=0, tiled=True),
        lax.all_gather(gain_attn, "shard", axis=0, tiled=True),
        lax.all_gather(shift_attn, "shard", axis=0, tiled=True),
        lax.all_gather(w_in, "shard", axis=0, tiled=True),
        lax.all_gather(bias_in, "shard", axis=0, tiled=True),
        lax.all_gather(w_back, "shard", axis=0, tiled=True),
        lax.all_gather(bias_back, "shard", axis=0, tiled=True),
        lax.all_gather(gain_ffn, "shard", axis=0, tiled=True),
        lax.all_gather(shift_ffn, "shard", axis=0, tiled=True),
    )
    f_qkv, f_bq, f_bv, f_out, f_bo, f_ga, f_sa, f_in, f_bi, f_back, f_bb, f_gf, f_sf = full
    group = lengths.shape[0]
    span = tokens.shape[0] // group
    width = tokens.shape[1]
    scale = HEAD_DIM ** (-0.5)
    factor = float(tokens.shape[0] * lax.axis_size("replica") * lax.axis_size("shard")) ** (-0.5)
    live = jnp.arange(span, dtype=jnp.int32)[None, :] < lengths[:, None]
    inputs = tokens.reshape(group, span, width)
    qkv = product("bld,de->ble", inputs, f_qkv)
    query = (qkv[..., :width] + f_bq.astype(f32)).astype(bf16).reshape(group, span, HEADS, HEAD_DIM)
    keys = qkv[..., width : 2 * width].astype(bf16).reshape(group, span, HEADS, HEAD_DIM)
    values = (
        (qkv[..., 2 * width :] + f_bv.astype(f32))
        .astype(bf16)
        .reshape(group, span, HEADS, HEAD_DIM)
    )

    def make_scores():
        raw = product("bqhe,bkhe->bhqk", query, keys) * scale
        return jnp.where(live[:, None, None, :], raw, -1000000000.0)

    scores = make_scores()
    top = jnp.max(scores, axis=-1, keepdims=True)
    expo = jnp.exp(scores - top)
    total = jnp.sum(expo, axis=-1, keepdims=True)
    log_total = top + jnp.log(total)
    attend = (expo / total).astype(bf16)
    context = product("bhqk,bkhe->bqhe", attend, values).reshape(group, span, width).astype(bf16)
    resid_one = inputs.astype(f32) + product("bld,de->ble", context, f_out) + f_bo.astype(f32)
    normed_one, inv_one = normalize(resid_one)
    gain_one = f_ga.astype(f32)
    mid = normed_one * gain_one + f_sa.astype(f32)
    mid_b = mid.astype(bf16)
    pre = product("bld,df->blf", mid_b, f_in) + f_bi.astype(f32)
    act = (0.5 * pre * (1.0 + lax.erf(pre * 0.7071067811865476))).astype(bf16)
    resid_two = mid + product("blf,fd->bld", act, f_back) + f_bb.astype(f32)
    normed_two, inv_two = normalize(resid_two)
    gain_two = f_gf.astype(f32)
    block_out = (normed_two * gain_two + f_sf.astype(f32)).astype(bf16)
    again = (
        lax.all_gather(w_qkv, "shard", axis=0, tiled=True),
        lax.all_gather(bias_q, "shard", axis=0, tiled=True),
        lax.all_gather(bias_v, "shard", axis=0, tiled=True),
        lax.all_gather(w_out, "shard", axis=0, tiled=True),
        lax.all_gather(bias_out, "shard", axis=0, tiled=True),
        lax.all_gather(gain_attn, "shard", axis=0, tiled=True),
        lax.all_gather(shift_attn, "shard", axis=0, tiled=True),
        lax.all_gather(w_in, "shard", axis=0, tiled=True),
        lax.all_gather(bias_in, "shard", axis=0, tiled=True),
        lax.all_gather(w_back, "shard", axis=0, tiled=True),
        lax.all_gather(bias_back, "shard", axis=0, tiled=True),
        lax.all_gather(gain_ffn, "shard", axis=0, tiled=True),
        lax.all_gather(shift_ffn, "shard", axis=0, tiled=True),
    )
    b_qkv = again[0]
    b_out = again[3]
    b_in = again[7]
    b_back = again[9]
    grad_out = cotangent.reshape(group, span, width).astype(f32) * live[..., None].astype(f32)
    g_gain_ffn = jnp.sum(grad_out * normed_two, axis=(0, 1))
    g_shift_ffn = jnp.sum(grad_out, axis=(0, 1))
    grad_two = norm_back(grad_out, normed_two, inv_two, gain_two)
    grad_two_b = grad_two.astype(bf16)
    g_w_back = product("blf,bld->fd", act, grad_two_b)
    g_bias_back = jnp.sum(grad_two, axis=(0, 1))
    grad_pre = product("bld,fd->blf", grad_two_b, b_back) * gelu_slope(pre)
    grad_pre_b = grad_pre.astype(bf16)
    g_w_in = product("bld,blf->df", mid_b, grad_pre_b)
    g_bias_in = jnp.sum(grad_pre, axis=(0, 1))
    grad_mid = grad_two + product("blf,df->bld", grad_pre_b, b_in)
    g_gain_attn = jnp.sum(grad_mid * normed_one, axis=(0, 1))
    g_shift_attn = jnp.sum(grad_mid, axis=(0, 1))
    grad_one = norm_back(grad_mid, normed_one, inv_one, gain_one)
    grad_one_b = grad_one.astype(bf16)
    g_w_out = product("bld,ble->de", context, grad_one_b)
    g_bias_out = jnp.sum(grad_one, axis=(0, 1))
    grad_ctx = (
        product("ble,de->bld", grad_one_b, b_out).astype(bf16).reshape(group, span, HEADS, HEAD_DIM)
    )
    weights_again = jnp.exp(make_scores() - log_total)
    weights_b = weights_again.astype(bf16)
    grad_att = product("bqhe,bkhe->bhqk", grad_ctx, values)
    grad_values = product("bhqk,bqhe->bkhe", weights_b, grad_ctx).reshape(group, span, width)
    delta = jnp.sum(weights_again * grad_att, axis=-1, keepdims=True)
    grad_scores = (weights_again * (grad_att - delta) * scale).astype(bf16)
    grad_query = product("bhqk,bkhe->bqhe", grad_scores, keys).reshape(group, span, width)
    grad_keys = product("bhqk,bqhe->bkhe", grad_scores, query).reshape(group, span, width)
    grad_qkv_b = jnp.concatenate([grad_query, grad_keys, grad_values], axis=-1).astype(bf16)
    g_w_qkv = product("bld,ble->de", inputs, grad_qkv_b)
    g_bias_q = jnp.sum(grad_query, axis=(0, 1))
    g_bias_v = jnp.sum(grad_values, axis=(0, 1))
    grad_input = grad_one + product("ble,de->bld", grad_qkv_b, b_qkv)
    shares = (
        lax.psum_scatter(g_w_qkv * factor, "shard", scatter_dimension=0, tiled=True),
        lax.psum_scatter(g_bias_q * factor, "shard", scatter_dimension=0, tiled=True),
        lax.psum_scatter(g_bias_v * factor, "shard", scatter_dimension=0, tiled=True),
        lax.psum_scatter(g_w_out * factor, "shard", scatter_dimension=0, tiled=True),
        lax.psum_scatter(g_bias_out * factor, "shard", scatter_dimension=0, tiled=True),
        lax.psum_scatter(g_gain_attn * factor, "shard", scatter_dimension=0, tiled=True),
        lax.psum_scatter(g_shift_attn * factor, "shard", scatter_dimension=0, tiled=True),
        lax.psum_scatter(g_w_in * factor, "shard", scatter_dimension=0, tiled=True),
        lax.psum_scatter(g_bias_in * factor, "shard", scatter_dimension=0, tiled=True),
        lax.psum_scatter(g_w_back * factor, "shard", scatter_dimension=0, tiled=True),
        lax.psum_scatter(g_bias_back * factor, "shard", scatter_dimension=0, tiled=True),
        lax.psum_scatter(g_gain_ffn * factor, "shard", scatter_dimension=0, tiled=True),
        lax.psum_scatter(g_shift_ffn * factor, "shard", scatter_dimension=0, tiled=True),
    )
    s_qkv, s_bq, s_bv, s_out, s_bo, s_ga, s_sa, s_in, s_bi, s_back, s_bb, s_gf, s_sf = shares
    summed = lax.psum(
        (s_qkv, s_bq, s_bv, s_out, s_bo, s_ga, s_sa, s_in, s_bi, s_back, s_bb, s_gf, s_sf),
        "replica",
    )
    r_qkv, r_bq, r_bv, r_out, r_bo, r_ga, r_sa, r_in, r_bi, r_back, r_bb, r_gf, r_sf = summed
    return (
        block_out.reshape(group * span, width),
        grad_input.reshape(group * span, width),
        r_qkv,
        r_bq,
        r_bv,
        r_out,
        r_bo,
        r_ga,
        r_sa,
        r_in,
        r_bi,
        r_back,
        r_bb,
        r_gf,
        r_sf,
    )


def solution(mesh):
    placed = (
        P(("replica", "shard"), None),
        P(("replica", "shard")),
        P(("replica", "shard"), None),
        P("shard", None),
        P("shard"),
        P("shard"),
        P("shard", None),
        P("shard"),
        P("shard"),
        P("shard"),
        P("shard", None),
        P("shard"),
        P("shard", None),
        P("shard"),
        P("shard"),
        P("shard"),
    )
    return jax.shard_map(
        on_device,
        mesh=mesh,
        in_specs=placed,
        out_specs=(
            P(("replica", "shard"), None),
            P(("replica", "shard"), None),
            P("shard", None),
            P("shard"),
            P("shard"),
            P("shard", None),
            P("shard"),
            P("shard"),
            P("shard"),
            P("shard", None),
            P("shard"),
            P("shard", None),
            P("shard"),
            P("shard"),
            P("shard"),
        ),
        check_vma=False,
    )
```

profile of v0, /device:TPU:0, one launch (start us, length us, event | category | flops | bytes accessed | tf_op | source)
XLA Modules:
  0.0 862.2 jit_solution(6676754043816239792)
XLA Ops:
  7.3 0.7 all-gather.14.cloned.1.call-update
  8.1 0.7 all-gather.16.cloned.1.call-update
  8.8 0.7 all-gather.18.cloned.1.call-update
  10.8 5.3 all-gather.1
  16.2 4.4 all-gather
  20.6 4.4 all-gather.2
  25.0 4.7 all-gather.3
  29.7 4.5 all-gather.4
  34.3 4.5 all-gather.6
  38.8 0.6 reshape.424
  39.4 4.5 all-gather.7
  44.0 4.5 all-gather.8
  48.5 0.6 reshape.426
  49.1 4.6 all-gather.5
  53.8 0.6 convert_element_type.147
  54.9 0.6 fusion.56
  55.5 6.5 all-gather.14.cloned.1.call-done
  62.0 3.1 convolution_bitcast_fusion
  65.3 0.9 copy.54
  66.2 1.0 copy.55
  67.2 0.9 copy.53
  68.1 1.9 fusion.63
  71.1 1.4 fusion.34
  72.5 13.8 %all-gather.16.cloned.1.call-done = bf16[768,768]{1,0:T(8,128)(2,1)} async-done(((bf16[384,768]{1,0:T(8,128)(2,1)}), bf16[768,768]{1,0:T(8,128)(2,1)}) %all-gather.16.cloned.1.call-update) | async-done | bytes 1179664 | tf_op jit(solution)/shard_map/all_gather | solution.py:61
  86.3 2.0 fusion.64
  88.3 0.9 copy-done
  89.4 0.6 add_rsqrt_fusion.1
  90.0 60.5 %all-gather.18.cloned.1.call-done = bf16[768,3072]{1,0:T(8,128)(2,1)} async-done(((bf16[384,3072]{1,0:T(8,128)(2,1)}), bf16[768,3072]{1,0:T(8,128)(2,1)}) %all-gather.18.cloned.1.call-update) | async-done | bytes 4718608 | tf_op jit(solution)/shard_map/all_gather | solution.py:65
  150.5 6.6 multiply_convert_fusion.1
  157.1 57.5 %all-gather.20.cloned.1.call-done = bf16[3072,768]{1,0:T(8,128)(2,1)} async-done(((bf16[1536,768]{1,0:T(8,128)(2,1)}), bf16[3072,768]{1,0:T(8,128)(2,1)}) %all-gather.20.cloned.1.call-update) | async-done | bytes 4718608 | tf_op jit(solution)/shard_map/all_gather | solution.py:67
  214.6 4.7 fusion.65
  219.5 1.0 multiply_reduce_fusion.1
  220.6 1.7 fusion.59
  222.3 3.0 fusion.68
  225.4 2.2 multiply_reduce_fusion.2
  227.7 0.9 fusion.60
  228.5 0.9 copy-done.3
  229.4 1.9 convolution_multiply_fusion.3
  231.6 1.4 log_add_fusion
  232.9 2.8 convolution_convert_fusion
  235.7 1.9 copy.57
  237.6 3.5 fusion.69
  241.1 5.1 fusion.35
  246.2 5.7 fusion.62
  251.9 1.8 fusion.61
  253.7 0.7 copy-done.9
  254.4 4.0 multiply_bitcast_fusion
  258.5 1.0 copy-done.2
  260.1 5.2 convolution_multiply_fusion.1
  265.3 1.1 copy-done.7
  266.4 0.6 copy-done.8
  267.0 5.1 convolution_multiply_fusion
  272.2 81.9 %reduce-scatter.5.cloned.1.call-done = f32[384,2304]{0,1:T(8,128)} async-done(((f32[768,2304]{0,1:T(8,128)}), f32[384,2304]{0,1:T(8,128)}) %reduce-scatter.5.cloned.1.call-update) | async-done | bytes 3538960 | tf_op jit(solution)/shard_map/reduce_scatter | solution.py:165
  354.1 113.0 %reduce-scatter.9.cloned.1.call-done = f32[384,3072]{1,0:T(8,128)} async-done(((f32[768,3072]{1,0:T(8,128)}), f32[384,3072]{1,0:T(8,128)}) %reduce-scatter.9.cloned.1.call-update) | async-done | bytes 4718608 | tf_op jit(solution)/shard_map/reduce_scatter | solution.py:172
  467.1 113.0 %reduce-scatter.11.cloned.1.call-done = f32[1536,768]{1,0:T(8,128)} async-done(((f32[3072,768]{1,0:T(8,128)}), f32[1536,768]{1,0:T(8,128)}) %reduce-scatter.11.cloned.1.call-update) | async-done | bytes 4718608 | tf_op jit(solution)/shard_map/reduce_scatter | solution.py:174
  580.7 0.6 dynamic-slice
  582.9 7.5 all-reduce.11
  591.0 62.7 %all-reduce.9 = (f32[384]{0:T(512)}, f32[384]{0:T(512)}, f32[384]{0:T(512)}, f32[384]{0:T(512)}, f32[384]{0:T(512)}, /*index=5*/f32[1536]{0:T(1024)}, f32[384]{0:T(512)}, f32[384]{0:T(512)}, f32[384]{0:T(512)}) all-reduce(f32[384]{0:T(512)S(1)} %dynamic-slice.1, ...), channel_id=1, replica_groups=mesh['replica'=16,'shard'=2] {'replica'}, use_global_device_ids=true, to_apply=%region_15.16 | all-reduce | flops 4608 | bytes 36864 | tf_op jit(solution)/shard_map/psum | solution.py:180
  653.8 4.1 convolution_add_fusion.2
  657.9 183.6 %all-reduce.14.cloned.1.call-done = (f32[384,2304]{0,1:T(8,128)}, f32[384,768]{1,0:T(8,128)}, f32[384,3072]{1,0:T(8,128)}, f32[1536,768]{1,0:T(8,128)}) async-done(((f32[384,2304]{0,1:T(8,128)}, f32[384,768]{1,0:T(8,128)}, f32[384,3072]{1,0:T(8,128)}, f32[1536,768]{1,0:T(8,128)}), (f32[384,2304]{0,1:T(8,128)}, f32[384,768]{1,0:T(8,128)}, f32[384,3072]{1,0:T(8,128)}, ...) | async-done | bytes 14155792 | tf_op jit(solution)/shard_map/psum | solution.py:180
  841.5 5.2 copy.61
  846.8 1.0 copy.71
  847.8 5.7 copy.72
  853.5 2.2 copy.73
  (175 shorter events, 5.7 us)
Async XLA Ops:
  7.2 3.6 copy-start.38
  7.2 8.9 %copy-start.39 = (bf16[384]{0:T(512)(128)(2,1)S(1)}, bf16[384]{0:T(512)(128)(2,1)}, u32[]{:S(2)}) copy-start(bf16[384]{0:T(512)(128)(2,1)} %param.21) | copy-start | bytes 2308
  7.2 13.3 %copy-start.40 = (bf16[384]{0:T(512)(128)(2,1)S(1)}, bf16[384]{0:T(512)(128)(2,1)}, u32[]{:S(2)}) copy-start(bf16[384]{0:T(512)(128)(2,1)} %param.23) | copy-start | bytes 2308
  7.2 17.8 %copy-start.41 = (bf16[384]{0:T(512)(128)(2,1)S(1)}, bf16[384]{0:T(512)(128)(2,1)}, u32[]{:S(2)}) copy-start(bf16[384]{0:T(512)(128)(2,1)} %param.24) | copy-start | bytes 2308
  7.2 22.5 %copy-start.42 = (bf16[384]{0:T(512)(128)(2,1)S(1)}, bf16[384]{0:T(512)(128)(2,1)}, u32[]{:S(2)}) copy-start(bf16[384]{0:T(512)(128)(2,1)} %param.25) | copy-start | bytes 2308
  7.2 54.8 %all-gather.14.cloned.1.call-start = ((), (), s32[]{:S(2)}) async-start(), calls=%async_computation.4 | async-start | bytes 5308416 | tf_op jit(solution)/shard_map/all_gather | solution.py:58
  8.0 26.3 %copy-start.43 = (bf16[384]{0:T(512)(128)(2,1)S(1)}, bf16[384]{0:T(512)(128)(2,1)}, u32[]{:S(2)}) copy-start(bf16[384]{0:T(512)(128)(2,1)} %param.29) | copy-start | bytes 2308
  8.0 31.4 %copy-start.44 = (bf16[384]{0:T(512)(128)(2,1)S(1)}, bf16[384]{0:T(512)(128)(2,1)}, u32[]{:S(2)}) copy-start(bf16[384]{0:T(512)(128)(2,1)} %param.30) | copy-start | bytes 2308
  8.0 36.0 %copy-start.45 = (bf16[384]{0:T(512)(128)(2,1)S(1)}, bf16[384]{0:T(512)(128)(2,1)}, u32[]{:S(2)}) copy-start(bf16[384]{0:T(512)(128)(2,1)} %param.31) | copy-start | bytes 2308
  8.0 41.1 %copy-start.34 = (bf16[1536]{0:T(1024)(128)(2,1)S(1)}, bf16[1536]{0:T(1024)(128)(2,1)}, u32[]{:S(2)}) copy-start(bf16[1536]{0:T(1024)(128)(2,1)} %param.27) | copy-start | bytes 9220
  8.0 54.0 %copy-start.5 = (bf16[256,768]{1,0:T(8,128)(2,1)S(1)}, bf16[256,768]{1,0:T(8,128)(2,1)}, u32[]{:S(2)}) copy-start(bf16[256,768]{1,0:T(8,128)(2,1)} %param.16) | copy-start | bytes 1179652
  8.0 78.3 %all-gather.16.cloned.1.call-start = ((), (), s32[]{:S(2)}) async-start(), calls=%async_computation.5 | async-start | bytes 1769472 | tf_op jit(solution)/shard_map/all_gather | solution.py:61
  8.8 141.8 %all-gather.18.cloned.1.call-start = ((), (), s32[]{:S(2)}) async-start(), calls=%async_computation.6 | async-start | bytes 7077888 | tf_op jit(solution)/shard_map/all_gather | solution.py:65
  9.5 205.1 %all-gather.20.cloned.1.call-start = ((), (), s32[]{:S(2)}) async-start(), calls=%async_computation.7 | async-start | bytes 7077888 | tf_op jit(solution)/shard_map/all_gather | solution.py:67
  10.1 262.1 %reduce-scatter.7.cloned.1.call-start = ((), (), s32[]{:S(2)}) async-start(), calls=%async_computation.9 | async-start | bytes 3538944 | tf_op jit(solution)/shard_map/reduce_scatter | solution.py:168
  68.1 3.0 copy-start.15
  70.0 0.6 copy-start.21
  70.5 0.6 copy-start.22
  88.3 0.9 copy-start
  88.3 139.3 %copy-start.23 = (f32[256]{0:T(256)}, f32[256]{0:T(256)S(1)}, u32[]{:S(2)}) copy-start(f32[256]{0:T(256)S(1)} %broadcast_multiply_fusion.14) | copy-start | bytes 3076
  214.6 7.7 slice-start.4
  214.6 4.9 copy-start.12
  214.6 4.9 copy-start.37
  214.6 6.0 copy-start.25
  214.6 7.7 slice-start.5
  219.3 3.0 copy-start.47
  220.6 4.8 slice-start.2
  222.3 3.1 copy-start.6
  222.3 3.0 copy-start.1
  222.3 3.0 copy-start.30
  222.3 3.0 slice-start.3
  225.3 2.3 copy-start.13
  225.4 4.0 copy-start.11
  228.5 0.9 copy-start.3
  231.3 122.8 %reduce-scatter.5.cloned.1.call-start = ((), (), s32[]{:S(2)}) async-start(), calls=%async_computation.8 | async-start | bytes 10616832 | tf_op jit(solution)/shard_map/reduce_scatter | solution.py:165
  251.9 2.5 copy-start.17
  251.9 2.5 copy-start.19
  253.7 0.8 copy-start.9
  258.4 1.1 copy-start.2
  258.4 1.7 copy-start.14
  258.4 1.7 copy-start.24
  258.4 1.7 copy-start.31
  258.4 208.6 %reduce-scatter.9.cloned.1.call-start = ((), (), s32[]{:S(2)}) async-start(), calls=%async_computation.10 | async-start | bytes 14155776 | tf_op jit(solution)/shard_map/reduce_scatter | solution.py:172
  265.2 1.2 copy-start.7
  265.3 1.7 copy-start.8
  265.3 314.8 %reduce-scatter.11.cloned.1.call-start = ((), (), s32[]{:S(2)}) async-start(), calls=%async_computation.11 | async-start | bytes 14155776 | tf_op jit(solution)/shard_map/reduce_scatter | solution.py:174
  272.1 569.4 %all-reduce.14.cloned.1.call-start = ((), (), s32[]{:S(2)}) async-start(), calls=%async_computation.12 | async-start | bytes 28311552 | tf_op jit(solution)/shard_map/psum | solution.py:180
  580.0 0.7 copy-start.46
  580.0 2.6 copy-start.33
  580.0 2.7 copy-start.36
  580.1 2.7 copy-start.26
  580.1 2.7 copy-start.27
  580.1 2.7 copy-start.35
  580.1 2.7 copy-start.28
  580.1 2.7 copy-start.29
  580.1 2.7 copy-start.32
  580.1 73.7 %copy-start.4 = (f32[256,768]{1,0:T(8,128)S(1)}, f32[256,768]{1,0:T(8,128)}, u32[]{:S(2)}) copy-start(f32[256,768]{1,0:T(8,128)} %copy-done.3) | copy-start | bytes 2359300
  580.1 73.7 %copy-start.10 = (bf16[1,256,12,64]{1,3,2,0:T(8,128)(2,1)S(1)}, bf16[1,256,12,64]{1,3,2,0:T(8,128)(2,1)}, u32[]{:S(2)}) copy-start(bf16[1,256,12,64]{1,3,2,0:T(8,128)(2,1)} %copy-done.9) | copy-start | bytes 1179652
  580.1 73.7 %copy-start.18 = (bf16[12,64,256]{2,1,0:T(8,128)(2,1)S(1)}, bf16[12,64,256]{2,1,0:T(8,128)(2,1)}, u32[]{:S(2)}) copy-start(bf16[12,64,256]{2,1,0:T(8,128)(2,1)} %fusion.35) | copy-start | bytes 1179652
  580.1 73.7 %copy-start.20 = (bf16[1,256,12,64]{1,3,2,0:T(8,128)(2,1)S(1)}, bf16[1,256,12,64]{1,3,2,0:T(8,128)(2,1)}, u32[]{:S(2)}) copy-start(bf16[1,256,12,64]{1,3,2,0:T(8,128)(2,1)} %get-tuple-element.100) | copy-start | bytes 1179652
  841.5 5.3 copy-start.16
  846.8 6.7 slice-start
  847.8 5.7 slice-start.1
Sparse Core Ops, SparseCore 0:
  9.6 52.3 all-gather.13
  63.5 22.7 all-gather.15
  87.9 62.6 all-gather.17
  151.9 62.6 all-gather.19
  231.4 34.7 reduce-scatter.6
  268.4 85.6 reduce-scatter.4
  356.4 110.6 reduce-scatter.8
  469.4 110.6 reduce-scatter.10
  584.6 256.8 all-reduce.13
where the time goes:
time: 863 us; the launch traced here: 862 us
  waiting for transfers between devices  632 us (73%)
  blocking collectives  112 us (13%)
  matrix products  64 us (7%)
  local copies, waits for them, and re-layouts  28.7 us (3%)
  between operations  16.4 us (2%)
    psum x1, waiting for transfers between devices, on_device(): lax.psum((s_qkv, s_bq, s_bv, s_out, s_bo, s_ga, s_sa, s_in, s_bi, s_back,...  184 us
    reduce_scatter x1, waiting for transfers between devices, on_device(): lax.psum_scatter(g_w_back * factor, 'shard', scatter_dimension=0, tiled=T...  113 us
    reduce_scatter x1, waiting for transfers between devices, on_device(): lax.psum_scatter(g_w_in * factor, 'shard', scatter_dimension=0, tiled=True)  113 us
    reduce_scatter x1, waiting for transfers between devices, on_device(): lax.psum_scatter(g_w_qkv * factor, 'shard', scatter_dimension=0, tiled=True)  81.9 us
    dot_general x18, matrix products, product(): return jnp.einsum(form, left, right, preferred_element_type=jnp.float32)  64 us
    psum x1, blocking collectives, on_device(): lax.psum((s_qkv, s_bq, s_bv, s_out, s_bo, s_ga, s_sa, s_in, s_bi, s_back,...  62.7 us
    all_gather x1, waiting for transfers between devices, on_device(): lax.all_gather(w_in, 'shard', axis=0, tiled=True)  60.5 us
    all_gather x1, waiting for transfers between devices, on_device(): lax.all_gather(w_back, 'shard', axis=0, tiled=True)  57.5 us
  transfers between devices with their start and end apart: 9, of which 8 were waited for; matrix products, arithmetic and copies ran while one was open for 7% of the time, Pallas kernels for 0%

commit v1 on v0

--- a/solution.py
+++ b/solution.py
@@ -64,7 +64,9 @@
         lax.all_gather(shift_attn, "shard", axis=0, tiled=True),
         lax.all_gather(w_in, "shard", axis=0, tiled=True),
         lax.all_gather(bias_in, "shard", axis=0, tiled=True),
-        lax.all_gather(w_back, "shard", axis=0, tiled=True),
+        jnp.concatenate(
+            lax.all_to_all(jnp.stack([w_back] * lax.axis_size("shard")), "shard", 0, 0), axis=0
+        ),
         lax.all_gather(bias_back, "shard", axis=0, tiled=True),
         lax.all_gather(gain_ffn, "shard", axis=0, tiled=True),
         lax.all_gather(shift_ffn, "shard", axis=0, tiled=True),

time: 863 us -> 899 us (1.042)
  blocking collectives: 112 us -> 198 us
  waiting for transfers between devices: 632 us -> 567 us
    all_gather x1, blocking collectives: 4.51 us -> 92 us  [on_device(): lax.all_gather(bias_back, 'shard', axis=0, tiled=True)]
    all_gather x1, waiting for transfers between devices: 60.5 us -> 24 us  [on_device(): lax.all_gather(w_in, 'shard', axis=0, tiled=True)]
    all_gather x1, waiting for transfers between devices: 13.8 us -> 0.01 us  [on_device(): lax.all_gather(w_out, 'shard', axis=0, tiled=True)]
    unnamed x131 -> x123, local copies, waits for them, and re-layouts: 22.5 us -> 22.5 us
  transfers between devices with their start and end apart: 9 -> 10, of which waited for: 8 -> 6; matrix products, arithmetic and copies ran while one was open for 7% -> 8% of each run, Pallas kernels for 0% -> 0%
where the time goes in v1:
time: 899 us; the launch traced here: 898 us
  waiting for transfers between devices  567 us (63%)
  blocking collectives  198 us (22%)
  matrix products  71.1 us (8%)
  local copies, waits for them, and re-layouts  28.7 us (3%)
  between operations  16.4 us (2%)
  other arithmetic  11.3 us (1%)
    psum x1, waiting for transfers between devices, on_device(): lax.psum((s_qkv, s_bq, s_bv, s_out, s_bo, s_ga, s_sa, s_in, s_bi, s_back,...  184 us
    reduce_scatter x1, waiting for transfers between devices, on_device(): lax.psum_scatter(g_w_back * factor, 'shard', scatter_dimension=0, tiled=T...  113 us
    reduce_scatter x1, waiting for transfers between devices, on_device(): lax.psum_scatter(g_w_in * factor, 'shard', scatter_dimension=0, tiled=True)  113 us
    all_gather x1, blocking collectives, on_device(): lax.all_gather(bias_back, 'shard', axis=0, tiled=True)  92 us
    reduce_scatter x1, waiting for transfers between devices, on_device(): lax.psum_scatter(g_w_qkv * factor, 'shard', scatter_dimension=0, tiled=True)  81.9 us
    dot_general x18, matrix products, product(): return jnp.einsum(form, left, right, preferred_element_type=jnp.float32)  71.1 us
    psum x1, blocking collectives, on_device(): lax.psum((s_qkv, s_bq, s_bv, s_out, s_bo, s_ga, s_sa, s_in, s_bi, s_back,...  62.8 us
    all_gather x1, waiting for transfers between devices, on_device(): lax.all_gather(w_back, 'shard', axis=0, tiled=True)  48.6 us
  transfers between devices with their start and end apart: 10, of which 6 were waited for; matrix products, arithmetic and copies ran while one was open for 8% of the time, Pallas kernels for 0%

profile of v1, /device:TPU:0, one launch (start us, length us, event | category | flops | bytes accessed | tf_op | source)
XLA Modules:
  0.0 898.5 jit_solution(4671556166196013117)
XLA Ops:
  7.2 0.7 all-gather.14.cloned.1.call-update
  8.0 0.7 all-gather.16.cloned.1.call-update
  8.7 0.7 all-gather.18.cloned.1.call-update
  9.4 2.6 pad_maximum_fusion
  12.1 5.9 all-to-all-start
  18.6 92.0 %all-gather.6 = bf16[2,1,384]{2,1,0:T(2,128)(2,1)S(1)} all-gather(bf16[1,1,384]{2,1,0:T(2,128)(2,1)S(1)} %reshape.416), channel_id=1, replica_groups=mesh['replica'=16,'shard'=2] {'shard'}, dimensions={0}, use_global_device_ids=true | all-gather | bytes 2304 | tf_op jit(solution)/shard_map/all_gather | solution.py:70
  110.6 0.6 reshape.428
  111.2 4.6 all-gather.5
  115.9 0.6 convert_element_type.147
  116.5 4.5 all-gather.2
  121.1 4.4 all-gather.1
  125.5 4.4 all-gather
  131.0 4.3 all-gather.4
  135.4 4.5 all-gather.3
  140.0 0.6 fusion.56
  140.6 4.5 all-gather.7
  145.1 4.5 all-gather.8
  149.7 0.6 reshape.430
  150.3 3.1 convolution_bitcast_fusion
  153.5 0.9 copy.53
  154.5 0.9 copy.54
  155.4 1.0 copy.55
  156.3 1.9 fusion.63
  159.3 1.4 fusion.34
  160.8 2.0 fusion.64
  162.8 0.9 copy-done
  163.9 0.6 add_rsqrt_fusion.1
  164.5 24.0 %all-gather.18.cloned.1.call-done = bf16[768,3072]{1,0:T(8,128)(2,1)} async-done(((bf16[384,3072]{1,0:T(8,128)(2,1)}), bf16[768,3072]{1,0:T(8,128)(2,1)}) %all-gather.18.cloned.1.call-update) | async-done | bytes 4718608 | tf_op jit(solution)/shard_map/all_gather | solution.py:65
  188.5 6.6 multiply_convert_fusion.1
  195.0 5.6 fusion.65
  200.9 1.0 multiply_reduce_fusion.1
  201.9 2.0 fusion.59
  203.9 48.6 %all-gather.20.cloned.1.call-done = bf16[3072,768]{1,0:T(8,128)(2,1)} async-done(((bf16[1536,768]{1,0:T(8,128)(2,1)}), bf16[3072,768]{1,0:T(8,128)(2,1)}) %all-gather.20.cloned.1.call-update) | async-done | bytes 4718608 | tf_op jit(solution)/shard_map/all_gather | solution.py:123
  252.5 6.1 fusion.68
  258.6 5.2 multiply_reduce_fusion.2
  263.9 0.9 fusion.60
  264.8 0.9 copy-done.4
  265.7 1.9 convolution_multiply_fusion.3
  267.8 1.3 log_add_fusion
  269.2 2.8 convolution_convert_fusion
  271.9 1.9 copy.57
  273.8 3.5 fusion.69
  277.4 5.1 fusion.35
  282.5 5.7 fusion.62
  288.2 1.8 fusion.61
  289.9 0.7 copy-done.10
  290.7 4.0 multiply_bitcast_fusion
  294.7 1.0 copy-done.2
  296.3 5.2 convolution_multiply_fusion.1
  301.6 1.1 copy-done.8
  302.7 0.6 copy-done.9
  303.2 5.1 convolution_multiply_fusion
  308.5 81.9 %reduce-scatter.5.cloned.1.call-done = f32[384,2304]{0,1:T(8,128)} async-done(((f32[768,2304]{0,1:T(8,128)}), f32[384,2304]{0,1:T(8,128)}) %reduce-scatter.5.cloned.1.call-update) | async-done | bytes 3538960 | tf_op jit(solution)/shard_map/reduce_scatter | solution.py:167
  390.4 113.0 %reduce-scatter.9.cloned.1.call-done = f32[384,3072]{1,0:T(8,128)} async-done(((f32[768,3072]{1,0:T(8,128)}), f32[384,3072]{1,0:T(8,128)}) %reduce-scatter.9.cloned.1.call-update) | async-done | bytes 4718608 | tf_op jit(solution)/shard_map/reduce_scatter | solution.py:174
  503.3 113.0 %reduce-scatter.11.cloned.1.call-done = f32[1536,768]{1,0:T(8,128)} async-done(((f32[3072,768]{1,0:T(8,128)}), f32[1536,768]{1,0:T(8,128)}) %reduce-scatter.11.cloned.1.call-update) | async-done | bytes 4718608 | tf_op jit(solution)/shard_map/reduce_scatter | solution.py:176
  617.0 0.6 dynamic-slice
  619.1 7.5 all-reduce.11
  627.3 62.8 %all-reduce.9 = (f32[384]{0:T(512)}, f32[384]{0:T(512)}, f32[384]{0:T(512)}, f32[384]{0:T(512)}, f32[384]{0:T(512)}, /*index=5*/f32[1536]{0:T(1024)}, f32[384]{0:T(512)}, f32[384]{0:T(512)}, f32[384]{0:T(512)}) all-reduce(f32[384]{0:T(512)S(1)} %dynamic-slice.1, ...), channel_id=1, replica_groups=mesh['replica'=16,'shard'=2] {'replica'}, use_global_device_ids=true, to_apply=%region_15.16 | all-reduce | flops 4608 | bytes 36864 | tf_op jit(solution)/shard_map/psum | solution.py:182
  690.1 4.1 convolution_add_fusion.2
  694.2 183.5 %all-reduce.14.cloned.1.call-done = (f32[384,2304]{0,1:T(8,128)}, f32[384,768]{1,0:T(8,128)}, f32[384,3072]{1,0:T(8,128)}, f32[1536,768]{1,0:T(8,128)}) async-done(((f32[384,2304]{0,1:T(8,128)}, f32[384,768]{1,0:T(8,128)}, f32[384,3072]{1,0:T(8,128)}, f32[1536,768]{1,0:T(8,128)}), (f32[384,2304]{0,1:T(8,128)}, f32[384,768]{1,0:T(8,128)}, f32[384,3072]{1,0:T(8,128)}, ...) | async-done | bytes 14155792 | tf_op jit(solution)/shard_map/psum | solution.py:182
  877.8 5.2 copy.61
  883.0 1.0 copy.71
  884.0 5.7 copy.72
  889.8 2.2 copy.73
  (168 shorter events, 5.7 us)
Async XLA Ops:
  7.2 2.2 copy-start.3
  7.2 143.1 %all-gather.14.cloned.1.call-start = ((), (), s32[]{:S(2)}) async-start(), calls=%async_computation.5 | async-start | bytes 5308416 | tf_op jit(solution)/shard_map/all_gather | solution.py:58
  7.9 152.9 %all-gather.16.cloned.1.call-start = ((), (), s32[]{:S(2)}) async-start(), calls=%async_computation.6 | async-start | bytes 1769472 | tf_op jit(solution)/shard_map/all_gather | solution.py:61
  8.7 179.8 %all-gather.18.cloned.1.call-start = ((), (), s32[]{:S(2)}) async-start(), calls=%async_computation.7 | async-start | bytes 7077888 | tf_op jit(solution)/shard_map/all_gather | solution.py:65
  12.0 6.6 copy-start.39
  12.0 99.2 %copy-start.35 = (bf16[1536]{0:T(1024)(128)(2,1)S(1)}, bf16[1536]{0:T(1024)(128)(2,1)}, u32[]{:S(2)}) copy-start(bf16[1536]{0:T(1024)(128)(2,1)} %param.27) | copy-start | bytes 9220
  12.0 104.5 %copy-start.40 = (bf16[384]{0:T(512)(128)(2,1)S(1)}, bf16[384]{0:T(512)(128)(2,1)}, u32[]{:S(2)}) copy-start(bf16[384]{0:T(512)(128)(2,1)} %param.23) | copy-start | bytes 2308
  12.0 109.0 %copy-start.41 = (bf16[384]{0:T(512)(128)(2,1)S(1)}, bf16[384]{0:T(512)(128)(2,1)}, u32[]{:S(2)}) copy-start(bf16[384]{0:T(512)(128)(2,1)} %param.20) | copy-start | bytes 2308
  12.0 113.4 %copy-start.42 = (bf16[384]{0:T(512)(128)(2,1)S(1)}, bf16[384]{0:T(512)(128)(2,1)}, u32[]{:S(2)}) copy-start(bf16[384]{0:T(512)(128)(2,1)} %param.21) | copy-start | bytes 2308
  12.0 119.0 %copy-start.43 = (bf16[384]{0:T(512)(128)(2,1)S(1)}, bf16[384]{0:T(512)(128)(2,1)}, u32[]{:S(2)}) copy-start(bf16[384]{0:T(512)(128)(2,1)} %param.25) | copy-start | bytes 2308
  12.0 123.4 %copy-start.44 = (bf16[384]{0:T(512)(128)(2,1)S(1)}, bf16[384]{0:T(512)(128)(2,1)}, u32[]{:S(2)}) copy-start(bf16[384]{0:T(512)(128)(2,1)} %param.24) | copy-start | bytes 2308
  12.1 128.5 %copy-start.45 = (bf16[384]{0:T(512)(128)(2,1)S(1)}, bf16[384]{0:T(512)(128)(2,1)}, u32[]{:S(2)}) copy-start(bf16[384]{0:T(512)(128)(2,1)} %param.30) | copy-start | bytes 2308
  12.1 133.0 %copy-start.46 = (bf16[384]{0:T(512)(128)(2,1)S(1)}, bf16[384]{0:T(512)(128)(2,1)}, u32[]{:S(2)}) copy-start(bf16[384]{0:T(512)(128)(2,1)} %param.31) | copy-start | bytes 2308
  12.1 138.2 %copy-start.6 = (bf16[256,768]{1,0:T(8,128)(2,1)S(1)}, bf16[256,768]{1,0:T(8,128)(2,1)}, u32[]{:S(2)}) copy-start(bf16[256,768]{1,0:T(8,128)(2,1)} %param.16) | copy-start | bytes 1179652
  12.1 182.9 %all-to-all-start = ((bf16[2,1536,768]{2,1,0:T(8,128)(2,1)}), bf16[2,1536,768]{2,1,0:T(8,128)(2,1)}, u32[]{:S(2)}, u32[]{:S(2)}) async-start(bf16[2,1536,768]{2,1,0:T(8,128)(2,1)} %pad_maximum_fusion), calls=%async_computation | async-start | bytes 9437184 | tf_op jit(solution)/shard_map/all_to_all | solution.py:68
  18.0 234.5 %all-gather.20.cloned.1.call-start = ((), (), s32[]{:S(2)}) async-start(), calls=%async_computation.8 | async-start | bytes 7077888 | tf_op jit(solution)/shard_map/all_gather | solution.py:123
  18.6 289.9 %reduce-scatter.7.cloned.1.call-start = ((), (), s32[]{:S(2)}) async-start(), calls=%async_computation.10 | async-start | bytes 3538944 | tf_op jit(solution)/shard_map/reduce_scatter | solution.py:170
  156.3 3.0 copy-start.16
  158.3 0.6 copy-start.22
  158.7 0.6 copy-start.23
  162.8 0.9 copy-start
  162.8 101.1 %copy-start.24 = (f32[256]{0:T(256)}, f32[256]{0:T(256)S(1)}, u32[]{:S(2)}) copy-start(f32[256]{0:T(256)S(1)} %broadcast_multiply_fusion.14) | copy-start | bytes 3076
  195.0 5.9 copy-start.13
  195.0 5.9 copy-start.38
  195.0 6.9 copy-start.26
  252.5 6.1 copy-start.1
  252.5 6.1 copy-start.7
  252.5 6.1 copy-start.31
  258.6 5.3 copy-start.14
  258.6 7.0 copy-start.12
  264.8 0.9 copy-start.4
  267.6 122.8 %reduce-scatter.5.cloned.1.call-start = ((), (), s32[]{:S(2)}) async-start(), calls=%async_computation.9 | async-start | bytes 10616832 | tf_op jit(solution)/shard_map/reduce_scatter | solution.py:167
  288.2 2.5 copy-start.18
  288.2 2.5 copy-start.20
  289.9 0.8 copy-start.10
  294.7 1.1 copy-start.2
  294.7 1.7 copy-start.15
  294.7 1.7 copy-start.25
  294.7 1.7 copy-start.32
  294.7 208.6 %reduce-scatter.9.cloned.1.call-start = ((), (), s32[]{:S(2)}) async-start(), calls=%async_computation.11 | async-start | bytes 14155776 | tf_op jit(solution)/shard_map/reduce_scatter | solution.py:174
  301.5 1.2 copy-start.8
  301.5 1.7 copy-start.9
  301.5 314.8 %reduce-scatter.11.cloned.1.call-start = ((), (), s32[]{:S(2)}) async-start(), calls=%async_computation.12 | async-start | bytes 14155776 | tf_op jit(solution)/shard_map/reduce_scatter | solution.py:176
  308.4 569.4 %all-reduce.14.cloned.1.call-start = ((), (), s32[]{:S(2)}) async-start(), calls=%async_computation.13 | async-start | bytes 28311552 | tf_op jit(solution)/shard_map/psum | solution.py:182
  616.3 0.7 copy-start.47
  616.3 2.5 copy-start.34
  616.3 2.7 copy-start.28
  616.3 2.7 copy-start.37
  616.3 2.7 copy-start.36
  616.3 2.7 copy-start.27
  616.3 2.7 copy-start.29
  616.3 2.7 copy-start.30
  616.3 2.8 copy-start.33
  616.4 73.7 %copy-start.5 = (f32[256,768]{1,0:T(8,128)S(1)}, f32[256,768]{1,0:T(8,128)}, u32[]{:S(2)}) copy-start(f32[256,768]{1,0:T(8,128)} %copy-done.4) | copy-start | bytes 2359300
  616.4 73.7 %copy-start.11 = (bf16[1,256,12,64]{1,3,2,0:T(8,128)(2,1)S(1)}, bf16[1,256,12,64]{1,3,2,0:T(8,128)(2,1)}, u32[]{:S(2)}) copy-start(bf16[1,256,12,64]{1,3,2,0:T(8,128)(2,1)} %copy-done.10) | copy-start | bytes 1179652
  616.4 73.7 %copy-start.19 = (bf16[12,64,256]{2,1,0:T(8,128)(2,1)S(1)}, bf16[12,64,256]{2,1,0:T(8,128)(2,1)}, u32[]{:S(2)}) copy-start(bf16[12,64,256]{2,1,0:T(8,128)(2,1)} %fusion.35) | copy-start | bytes 1179652
  616.4 73.7 %copy-start.21 = (bf16[1,256,12,64]{1,3,2,0:T(8,128)(2,1)S(1)}, bf16[1,256,12,64]{1,3,2,0:T(8,128)(2,1)}, u32[]{:S(2)}) copy-start(bf16[1,256,12,64]{1,3,2,0:T(8,128)(2,1)} %get-tuple-element.100) | copy-start | bytes 1179652
  877.8 5.3 copy-start.17
  883.0 6.7 slice-start
  884.0 5.7 slice-start.1
Sparse Core Ops, SparseCore 0:
  9.5 90.0 all-gather.13
  101.2 22.9 all-gather.15
  125.7 62.6 all-gather.17
  189.8 62.6 all-gather.19
  267.7 34.7 reduce-scatter.6
  304.7 85.6 reduce-scatter.4
  392.7 110.6 reduce-scatter.8
  505.6 110.6 reduce-scatter.10
  620.9 256.8 all-reduce.13
